TPU v7x, 32 devices: a whole 2x2x4 slice. The times are simulated.
32 devices in a mesh: grp: 2 (over core), blk: 16 (over z, y, x).
Axes of the slice: x: 2, y: 2, z: 4, core: 2. Of those that a mesh axis runs over, the one named last changes fastest.
Arguments:
- nullspace: float32 [6, 65536], P(None, ('grp', 'blk')), may hold values from -6 to 6
- agg_ids: int32 [65536], P(('grp', 'blk')), may hold values from 0 to 1535
- nbr_index: int32 [8, 65536], P(None, ('grp', 'blk')), may hold values from 0 to 6143
- nbr_weight: float32 [8, 65536], P(None, ('grp', 'blk')), may hold values from -0.25 to 0.25
Outputs:
- factor: float32 [21, 3072], P(None, ('grp', 'blk'))
- spread: float32 [3072], P(('grp', 'blk'))
All inputs are finite; a program needn't handle non-finite values.
Results may differ from a plain program's by a relative error of at most 0.000088.
Values sent between devices are 32-bit elements; how exact they have to be, the bound alone decides.
No kernel may reach another device: no remote copies, remote signals or barrier semaphores. Data moves between devices by JAX's collectives and lax.ppermute only.
A program may use at most 64 MiB of HBM per device.

v0:
```python
import jax
import jax.numpy as jnp
from jax import lax
from jax.sharding import PartitionSpec as P

ROWS_DEV = 2048
AGG_DEV = 96


def with_halo(cells, sides, width):
    for axis, dim in sides:
        count = lax.axis_size(axis)
        ends = count - 1
        head = lax.slice_in_dim(cells, 0, width, axis=dim)
        tail = lax.slice_in_dim(cells, cells.shape[dim] - width, cells.shape[dim], axis=dim)
        cells = jnp.concatenate(
            [
                lax.ppermute(tail, axis, [(i, (i + 1) % count) for i in range(ends)]),
                cells,
                lax.ppermute(head, axis, [((i + 1) % count, i) for i in range(ends)]),
            ],
            axis=dim,
        )
    return cells


def pair_list():
    return [(p, q) for p in range(6) for q in range(p, 6)]


def factorize(packed):
    pairs = pair_list()
    entry = {}
    for idx, (p, q) in enumerate(pairs):
        entry[p, q] = packed[idx]
        entry[q, p] = packed[idx]
    lower = {}
    for j in range(6):
        total = entry[j, j]
        for k in range(j):
            total = total - lower[j, k] * lower[j, k]
        diag = jnp.sqrt(total)
        lower[j, j] = diag
        for i in range(j + 1, 6):
            total = entry[i, j]
            for k in range(j):
                total = total - lower[i, k] * lower[j, k]
            lower[i, j] = total / diag
    factor = jnp.stack([lower[q, p] for p, q in pairs], axis=0)
    diags = jnp.stack([lower[j, j] for j in range(6)], axis=0)
    spread = jnp.log(jnp.max(diags, axis=0)) - jnp.log(jnp.min(diags, axis=0))
    return (factor, spread)


def shards(nullspace, agg_ids, nbr_index, nbr_weight):
    vectors, rows = nullspace.shape
    neighbours = nbr_index.shape[0]
    padded = with_halo(nullspace[None], (("grp", 0),), 1)
    extended = jnp.transpose(padded, (1, 0, 2)).reshape(vectors, 3 * rows)
    ext_cols = jnp.arange(3 * rows, dtype=jnp.int32)
    blocks_blk = lax.axis_size("blk")
    group_aggs = AGG_DEV * blocks_blk
    block_rows = min(512, rows)
    count_blocks = rows // block_rows
    null_blocks = jnp.transpose(nullspace.reshape(vectors, count_blocks, block_rows), (1, 0, 2))
    index_blocks = jnp.transpose(nbr_index.reshape(neighbours, count_blocks, block_rows), (1, 0, 2))
    weight_blocks = jnp.transpose(
        nbr_weight.reshape(neighbours, count_blocks, block_rows), (1, 0, 2)
    )
    id_blocks = agg_ids.reshape(count_blocks, block_rows)
    columns = jnp.arange(group_aggs, dtype=jnp.int32)
    pairs = pair_list()

    def accumulate(total, inputs):
        null_part, index_part, weight_part, id_part = inputs
        mixing = jnp.zeros((block_rows, 3 * rows), jnp.float32)
        for k in range(neighbours):
            mixing = mixing + jnp.where(
                index_part[k][:, None] == ext_cols[None, :], weight_part[k][:, None], 0.0
            )
        nearby = lax.dot_general(
            extended,
            mixing,
            (((1,), (1,)), ((), ())),
            precision=lax.Precision.HIGHEST,
            preferred_element_type=jnp.float32,
        )
        smoothed = null_part - nearby
        terms = jnp.stack([smoothed[p] * smoothed[q] for p, q in pairs], axis=0)
        one_hot = (id_part[:, None] == columns[None, :]).astype(jnp.float32)
        total = total + jnp.dot(
            terms, one_hot, precision=lax.Precision.HIGHEST, preferred_element_type=jnp.float32
        )
        return (total, None)

    start_total = jnp.zeros((len(pairs), group_aggs), jnp.float32)
    partial_gram, _ = lax.scan(
        accumulate, start_total, (null_blocks, index_blocks, weight_blocks, id_blocks)
    )
    whole = lax.psum(partial_gram, "blk")
    offset = lax.axis_index("blk") * AGG_DEV
    mine = lax.dynamic_slice_in_dim(whole, offset, AGG_DEV, 1)
    identity = jnp.array([1.0 if p == q else 0.0 for p, q in pairs], jnp.float32)
    gram = mine * (AGG_DEV / ROWS_DEV) + identity[:, None]
    return factorize(gram)


def solution(mesh):
    return jax.shard_map(
        shards,
        mesh=mesh,
        in_specs=(
            P(None, ("grp", "blk")),
            P(("grp", "blk")),
            P(None, ("grp", "blk")),
            P(None, ("grp", "blk")),
        ),
        out_specs=(P(None, ("grp", "blk")), P(("grp", "blk"))),
        check_vma=False,
    )
```

profile of v0, /device:TPU:0, one launch (start us, length us, event | category | flops | bytes accessed | tf_op | source)
XLA Modules:
  0.0 279.0 jit_solution(1921388014540714053)
XLA Ops:
  7.2 2.4 collective-permute-start
  9.6 1.3 collective-permute-start.1
  10.9 0.7 reshape.96
  11.6 1.3 collective-permute-done.1
  13.0 0.9 pad_maximum_fusion
  13.9 145.3 %while.12 = (s32[]{:T(128)}, f32[21,1536]{1,0:T(8,128)S(1)}, f32[4,6,512]{2,1,0:T(8,128)}, s32[4,8,512]{2,1,0:T(8,128)}, f32[4,8,512]{2,1,0:T(8,128)}, /*index=5...) while((s32[]{:T(128)}, f32[21,1536]{1,0:T(8,128)S(1)}, ...), condition=%wide.region_1.2_spmd.clone.clone, body=%wide.region_0.1_spmd.clone.clone.sunk | while | flops 497889792 | bytes 25895224 | solution.py:97
  13.9 1.0 constant_dynamic-slice_fusion.20
  14.9 1.0 constant_dynamic-slice_fusion.21
  16.0 21.4 %fusion.81 = f32[512,6144]{1,0:T(8,128)S(1)} fusion(f32[512]{0:T(512)S(1)} %bitcast.100, s32[512]{0:T(512)S(1)} %bitcast.108, f32[512]{0:T(512)S(1)} %bitcast.94, s32[512]{0:T(512)S(1)} %bitcast.102, f32[512]{0:T(512)S(1)} %bitcast.95, s32[512]{0:T(512)S(1)} %bitcast.103, f32[512]{0:T(512)S(1)} %bitcast.96, ...), kind=kLoop, calls=%fused_computation.11.clone.clone.clone.clone.clone.1.clone.1 | loop fusion | flops 72351744 | bytes 12615680 | tf_op jit(solution)/shard_map/while/body/eval_jaxpr/dot_general | solution.py:81
  37.4 11.4 %fusion.82 = f32[6,512]{1,0:T(8,128)S(1)} fusion(f32[6,6144]{1,0:T(8,128)S(1)} %get-tuple-element.373, f32[4,6,512]{2,1,0:T(8,128)} %get-tuple-element.370, s32[]{:T(128)} %get-tuple-element.352, f32[512,6144]{1,0:T(8,128)S(1)} %fusion.81), kind=kOutput, calls=%fused_computation.48.clone.2 | convolution fusion | flops 226495488 | bytes 12754948 | tf_op jit(solution)/shard_map/while/body/eval_jaxpr/dot_general | solution.py:81
  49.0 1.2 fusion.83
  50.2 1.0 constant_dynamic-slice_fusion.20
  51.2 1.0 constant_dynamic-slice_fusion.21
  52.3 21.4 %fusion.81 = f32[512,6144]{1,0:T(8,128)S(1)} fusion(f32[512]{0:T(512)S(1)} %bitcast.100, s32[512]{0:T(512)S(1)} %bitcast.108, f32[512]{0:T(512)S(1)} %bitcast.94, s32[512]{0:T(512)S(1)} %bitcast.102, f32[512]{0:T(512)S(1)} %bitcast.95, s32[512]{0:T(512)S(1)} %bitcast.103, f32[512]{0:T(512)S(1)} %bitcast.96, ...), kind=kLoop, calls=%fused_computation.11.clone.clone.clone.clone.clone.1.clone.1 | loop fusion | flops 72351744 | bytes 12615680 | tf_op jit(solution)/shard_map/while/body/eval_jaxpr/dot_general | solution.py:81
  73.7 11.4 %fusion.82 = f32[6,512]{1,0:T(8,128)S(1)} fusion(f32[6,6144]{1,0:T(8,128)S(1)} %get-tuple-element.373, f32[4,6,512]{2,1,0:T(8,128)} %get-tuple-element.370, s32[]{:T(128)} %get-tuple-element.352, f32[512,6144]{1,0:T(8,128)S(1)} %fusion.81), kind=kOutput, calls=%fused_computation.48.clone.2 | convolution fusion | flops 226495488 | bytes 12754948 | tf_op jit(solution)/shard_map/while/body/eval_jaxpr/dot_general | solution.py:81
  85.2 0.1 stack.8
  85.3 1.2 fusion.83
  86.5 1.0 constant_dynamic-slice_fusion.20
  87.6 1.0 constant_dynamic-slice_fusion.21
  88.6 21.4 %fusion.81 = f32[512,6144]{1,0:T(8,128)S(1)} fusion(f32[512]{0:T(512)S(1)} %bitcast.100, s32[512]{0:T(512)S(1)} %bitcast.108, f32[512]{0:T(512)S(1)} %bitcast.94, s32[512]{0:T(512)S(1)} %bitcast.102, f32[512]{0:T(512)S(1)} %bitcast.95, s32[512]{0:T(512)S(1)} %bitcast.103, f32[512]{0:T(512)S(1)} %bitcast.96, ...), kind=kLoop, calls=%fused_computation.11.clone.clone.clone.clone.clone.1.clone.1 | loop fusion | flops 72351744 | bytes 12615680 | tf_op jit(solution)/shard_map/while/body/eval_jaxpr/dot_general | solution.py:81
  110.0 11.4 %fusion.82 = f32[6,512]{1,0:T(8,128)S(1)} fusion(f32[6,6144]{1,0:T(8,128)S(1)} %get-tuple-element.373, f32[4,6,512]{2,1,0:T(8,128)} %get-tuple-element.370, s32[]{:T(128)} %get-tuple-element.352, f32[512,6144]{1,0:T(8,128)S(1)} %fusion.81), kind=kOutput, calls=%fused_computation.48.clone.2 | convolution fusion | flops 226495488 | bytes 12754948 | tf_op jit(solution)/shard_map/while/body/eval_jaxpr/dot_general | solution.py:81
  121.7 1.2 fusion.83
  122.8 1.0 constant_dynamic-slice_fusion.20
  123.9 1.0 constant_dynamic-slice_fusion.21
  124.9 21.4 %fusion.81 = f32[512,6144]{1,0:T(8,128)S(1)} fusion(f32[512]{0:T(512)S(1)} %bitcast.100, s32[512]{0:T(512)S(1)} %bitcast.108, f32[512]{0:T(512)S(1)} %bitcast.94, s32[512]{0:T(512)S(1)} %bitcast.102, f32[512]{0:T(512)S(1)} %bitcast.95, s32[512]{0:T(512)S(1)} %bitcast.103, f32[512]{0:T(512)S(1)} %bitcast.96, ...), kind=kLoop, calls=%fused_computation.11.clone.clone.clone.clone.clone.1.clone.1 | loop fusion | flops 72351744 | bytes 12615680 | tf_op jit(solution)/shard_map/while/body/eval_jaxpr/dot_general | solution.py:81
  146.4 11.4 %fusion.82 = f32[6,512]{1,0:T(8,128)S(1)} fusion(f32[6,6144]{1,0:T(8,128)S(1)} %get-tuple-element.373, f32[4,6,512]{2,1,0:T(8,128)} %get-tuple-element.370, s32[]{:T(128)} %get-tuple-element.352, f32[512,6144]{1,0:T(8,128)S(1)} %fusion.81), kind=kOutput, calls=%fused_computation.48.clone.2 | convolution fusion | flops 226495488 | bytes 12754948 | tf_op jit(solution)/shard_map/while/body/eval_jaxpr/dot_general | solution.py:81
  158.0 1.2 fusion.83
  159.2 0.6 copy-done
  159.9 109.0 %all-reduce.2.cloned.1.call-done = f32[21,1536]{1,0:T(8,128)} async-done(((f32[21,1536]{1,0:T(8,128)}), f32[21,1536]{1,0:T(8,128)}) %all-reduce.2.cloned.1.call-update) | async-done | bytes 129040 | tf_op jit(solution)/shard_map/psum | solution.py:100
  268.8 0.8 multiply_add_fusion
  269.7 0.6 subtract_bitcast_fusion
  270.3 1.8 stack.4
  (26 shorter events, 0.7 us)
Async XLA Ops:
  7.2 261.6 %all-reduce.2.cloned.1.call-start = ((), (), s32[]{:S(2)}) async-start(), calls=%async_computation | async-start | bytes 294912 | tf_op jit(solution)/shard_map/psum | solution.py:100
  7.2 4.4 %collective-permute-start = (f32[1,6,2048]{2,1,0:T(8,128)}, f32[1,6,2048]{2,1,0:T(8,128)S(1)}, u32[]{:S(2)}, u32[]{:S(2)}) collective-permute-start(f32[1,6,2048]{2,1,0:T(8,128)} %bitcast.89), channel_id=1, source_target_pairs={{0,16},{1,17},{2,18},{3,19},{4,20},{5,21},{6,22},{7,23},{8,24},{9,... | collective-permute-start | bytes 147464 | tf_op jit(solution)/shard_map/ppermute | solution.py:18
  9.6 3.4 %collective-permute-start.1 = (f32[1,6,2048]{2,1,0:T(8,128)}, f32[1,6,2048]{2,1,0:T(8,128)S(1)}, u32[]{:S(2)}, u32[]{:S(2)}) collective-permute-start(f32[1,6,2048]{2,1,0:T(8,128)} %bitcast.90), channel_id=1, source_target_pairs={{16,0},{17,1},{18,2},{19,3},{20,4},{21,5},{22,6},{23,7},{24,8},{25... | collective-permute-start | bytes 147464 | tf_op jit(solution)/shard_map/ppermute | solution.py:20
  13.8 255.0 %copy-start.1 = (f32[21]{0:T(128)S(1)}, f32[21]{0:T(128)}, u32[]{:S(2)}) copy-start(f32[21]{0:T(128)} %constant.22.clone) | copy-start | bytes 256
  159.2 0.7 copy-start
Sparse Core Ops, SparseCore 0:
  160.0 108.7 all-reduce.1
where the time goes:
time: 280 us; the launch traced here: 279 us
  waiting for transfers between devices  110 us (39%)
  other arithmetic  88.2 us (32%)
  matrix products  50.4 us (18%)
  between operations  14.1 us (5%)
  local copies, waits for them, and re-layouts  12 us (4%)
  starting transfers between devices  3.73 us (1%)
    psum x1, waiting for transfers between devices, shards(): whole = lax.psum(partial_gram, 'blk')  109 us
    dot_general x4, other arithmetic, accumulate(): lax.dot_general(extended, mixing, (((1,), (1,)), ((), ())), precision=lax...  85.7 us
    dot_general x4, matrix products, accumulate(): lax.dot_general(extended, mixing, (((1,), (1,)), ((), ())), precision=lax...  45.7 us
  transfers between devices with their start and end apart: 3, of which 2 were waited for; matrix products, arithmetic and copies ran while one was open for 0% of the time, Pallas kernels for 0%

commit v1 on v0

v1 whole, which is shorter than its diff:
```python
import functools

import jax
import jax.numpy as jnp
from jax import lax
from jax.experimental import pallas as pl
from jax.experimental.pallas import tpu as pltpu
from jax.sharding import PartitionSpec as P

ROWS_DEV = 2048
AGG_DEV = 96
LANES = 128


def pair_list(vectors):
    return [(p, q) for p in range(vectors) for q in range(p, vectors)]


def share_of(ids, shares):
    shift = 22
    factor = -(-(1 << shift) // AGG_DEV)
    most = shares * AGG_DEV - 1
    assert most * factor < 2**31 and (factor * AGG_DEV - (1 << shift)) * most < (1 << shift)
    return lax.shift_right_logical(ids * factor, shift)


def gram_kernel(shares, own_ref, *refs):
    *others, ids_ref, index_ref, weight_ref, out_ref = refs
    vectors, rows = own_ref.shape
    pairs = pair_list(vectors)
    padded = out_ref.shape[1]
    tables = [(own_ref, rows)]
    for table_ref, start_ref in zip(others[0::2], others[1::2]):
        tables.append((table_ref, start_ref[0]))
    gram = [jnp.zeros((shares * padded, AGG_DEV), jnp.float32) for _ in range(2)]
    step = 2 * LANES
    for first in range(0, rows, step):
        pieces = []
        for start in range(first, first + step, LANES):
            here = slice(start, start + LANES)
            index = index_ref[:, here]
            weight = weight_ref[:, here]
            low = jnp.bitwise_and(index, LANES - 1)
            picked = [jnp.zeros(index.shape, jnp.float32) for _ in range(vectors)]
            for table_ref, base in tables:
                high = lax.shift_right_arithmetic(index - base, 7)
                for chunk in range(rows // LANES):
                    found = high == chunk
                    for v in range(vectors):
                        row = table_ref[v : v + 1, chunk * LANES : (chunk + 1) * LANES]
                        value = jnp.take_along_axis(
                            jnp.broadcast_to(row, index.shape), low, axis=1, mode="promise_in_bounds"
                        )
                        picked[v] = jnp.where(found, value, picked[v])
            smooth = [
                own_ref[v : v + 1, here] - jnp.sum(weight * picked[v], axis=0, keepdims=True)
                for v in range(vectors)
            ]
            pieces.append([smooth[p] * smooth[q] for p, q in pairs])
        zero = jnp.zeros((padded - len(pairs), step), jnp.float32)
        terms = jnp.concatenate(
            [jnp.concatenate([half[i] for half in pieces], axis=1) for i in range(len(pairs))] + [zero],
            axis=0,
        )
        coarse = terms.astype(jnp.bfloat16).astype(jnp.float32)
        ids = ids_ref[:, first : first + step]
        share = share_of(ids, shares)
        within = ids - share * AGG_DEV
        lanes = lax.broadcasted_iota(jnp.int32, (AGG_DEV, step), 0)
        one_hot = (lanes == within).astype(jnp.float32).astype(jnp.bfloat16)
        for piece, part in enumerate((coarse, terms - coarse)):
            spread_out = jnp.concatenate(
                [jnp.where(share == s, part, 0.0) for s in range(shares)], axis=0
            ).astype(jnp.bfloat16)
            gram[piece] = gram[piece] + lax.dot_general(
                spread_out, one_hot, (((1,), (1,)), ((), ())), preferred_element_type=jnp.float32
            )
    out_ref[...] = (gram[0] + gram[1]).reshape(out_ref.shape)


def factor_kernel(vectors, parts_ref, factor_ref, spread_ref):
    pairs = pair_list(vectors)
    total = parts_ref[0]
    for source in range(1, parts_ref.shape[0]):
        total = total + parts_ref[source]
    entry = {}
    for i, (p, q) in enumerate(pairs):
        value = total[i : i + 1] * (AGG_DEV / ROWS_DEV)
        entry[p, q] = value + 1.0 if p == q else value
    upper = {}
    for j in range(vectors):
        pivot = entry[j, j]
        for k in range(j):
            pivot = pivot - upper[k, j] * upper[k, j]
        upper[j, j] = jnp.sqrt(pivot)
        for i in range(j + 1, vectors):
            rest = entry[j, i]
            for k in range(j):
                rest = rest - upper[k, i] * upper[k, j]
            upper[j, i] = rest / upper[j, j]
    for i, pair in enumerate(pairs):
        factor_ref[i : i + 1, :] = upper[pair]
    most = functools.reduce(jnp.maximum, [upper[j, j] for j in range(vectors)])
    least = functools.reduce(jnp.minimum, [upper[j, j] for j in range(vectors)])
    spread_ref[...] = jnp.log(most) - jnp.log(least)


def shards(nullspace, agg_ids, nbr_index, nbr_weight):
    vectors, rows = nullspace.shape
    groups, shares = lax.axis_size("grp"), lax.axis_size("blk")
    pairs = pair_list(vectors)
    padded = -(-len(pairs) // 8) * 8
    vmem = pl.BlockSpec(memory_space=pltpu.VMEM)
    smem = pl.BlockSpec(memory_space=pltpu.SMEM)
    if groups == 2:
        other = lax.ppermute(nullspace, "grp", [(0, 1), (1, 0)])
        start = (2 * rows * (1 - lax.axis_index("grp"))).astype(jnp.int32).reshape(1)
        tables = [other, start]
    else:
        before = lax.ppermute(nullspace, "grp", [(i, i + 1) for i in range(groups - 1)])
        after = lax.ppermute(nullspace, "grp", [(i + 1, i) for i in range(groups - 1)])
        tables = [
            before,
            jnp.zeros((1,), jnp.int32),
            after,
            jnp.full((1,), 2 * rows, jnp.int32),
        ]
    partial = pl.pallas_call(
        functools.partial(gram_kernel, shares),
        out_shape=jax.ShapeDtypeStruct((shares, padded, AGG_DEV), jnp.float32),
        in_specs=[vmem] + [vmem, smem] * (len(tables) // 2) + [vmem] * 3,
        out_specs=vmem,
        name="gram",
    )(nullspace, *tables, agg_ids.reshape(1, rows), nbr_index, nbr_weight)
    parts = lax.all_to_all(partial, "blk", 0, 0, tiled=True)
    factor, spread = pl.pallas_call(
        functools.partial(factor_kernel, vectors),
        out_shape=(
            jax.ShapeDtypeStruct((len(pairs), AGG_DEV), jnp.float32),
            jax.ShapeDtypeStruct((1, AGG_DEV), jnp.float32),
        ),
        in_specs=[vmem],
        out_specs=(vmem, vmem),
        name="factor",
    )(parts)
    return factor, spread.reshape(AGG_DEV)


def solution(mesh):
    return jax.shard_map(
        shards,
        mesh=mesh,
        in_specs=(
            P(None, ("grp", "blk")),
            P(("grp", "blk")),
            P(None, ("grp", "blk")),
            P(None, ("grp", "blk")),
        ),
        out_specs=(P(None, ("grp", "blk")), P(("grp", "blk"))),
        check_vma=False,
    )
```

time: 280 us -> 27.6 us (0.10)
  waiting for transfers between devices: 110 us -> 1.11 us
  other arithmetic: 88.2 us -> 0 us
  matrix products: 50.4 us -> 0 us
  blocking collectives: 0 us -> 17.3 us
  between operations: 14.1 us -> 0.63 us
  local copies, waits for them, and re-layouts: 12 us -> 0.62 us
  Pallas kernels: 0 us -> 7.13 us
  starting transfers between devices: 3.73 us -> 0.56 us
    psum x1 -> x0, waiting for transfers between devices: 109 us -> none  [shards(): whole = lax.psum(partial_gram, 'blk')]
    dot_general x4 -> x0, other arithmetic: 85.7 us -> none  [accumulate(): lax.dot_general(extended, mixing, (((1,), (1,)), ((), ())), precision=lax...]
    dot_general x8 -> x0, matrix products: 50.4 us -> none  [the longest x4 45.7 us: accumulate(): lax.dot_general(extended, mixing, (((1,), (1,)), ((), ())), precision=lax...]
    all_to_all x0 -> x1, blocking collectives: none -> 17.3 us  [shards(): parts = lax.all_to_all(partial, 'blk', 0, 0, tiled=True)]
    slice x8 -> x0, local copies, waits for them, and re-layouts: 8.32 us -> none  [the longest x4 4.17 us: accumulate(): index_part[k][:, None] == ext_cols[None, :]]
    pallas_call x0 -> x2, Pallas kernels: none -> 7.13 us  [the longest x1 5.48 us: shards(): pl.pallas_call(functools.partial(gram_kernel, shares), out_shape=jax.Shap...]
    ppermute x2 -> x1, starting transfers between devices: 3.69 us -> 0.56 us  [shards(): other = lax.ppermute(nullspace, 'grp', [(0, 1), (1, 0)])]
  transfers between devices with their start and end apart: 3 -> 1, of which waited for: 2 -> 1; matrix products, arithmetic and copies ran while one was open for 0% -> 0% of each run, Pallas kernels for 0% -> 0%
where the time goes in v1:
time: 27.6 us; the launch traced here: 27.3 us
  blocking collectives  17.3 us (63%)
  Pallas kernels  7.13 us (26%)
  waiting for transfers between devices  1.11 us (4%)
  between operations  0.63 us (2%)
  local copies, waits for them, and re-layouts  0.62 us (2%)
  starting transfers between devices  0.56 us (2%)
    all_to_all x1, blocking collectives, shards(): parts = lax.all_to_all(partial, 'blk', 0, 0, tiled=True)  17.3 us
    pallas_call x1, Pallas kernels, shards(): pl.pallas_call(functools.partial(gram_kernel, shares), out_shape=jax.Shap...  5.48 us
    pallas_call x1, Pallas kernels, shards(): pl.pallas_call(functools.partial(factor_kernel, vectors), out_shape=(jax....  1.65 us
    ppermute x1, waiting for transfers between devices, shards(): other = lax.ppermute(nullspace, 'grp', [(0, 1), (1, 0)])  1.11 us
    unnamed x2, local copies, waits for them, and re-layouts  0.62 us
    ppermute x1, starting transfers between devices, shards(): other = lax.ppermute(nullspace, 'grp', [(0, 1), (1, 0)])  0.56 us
  transfers between devices with their start and end apart: 1, of which 1 were waited for; matrix products, arithmetic and copies ran while one was open for 0% of the time, Pallas kernels for 0%

profile of v1, /device:TPU:0, one launch (start us, length us, event | category | flops | bytes accessed | tf_op | source)
XLA Modules:
  0.0 27.3 jit_solution(5489631885529397193)
XLA Ops:
  0.6 0.6 %collective-permute-start = (f32[6,2048]{1,0:T(8,128)}, f32[6,2048]{1,0:T(8,128)S(1)}, u32[]{:S(2)}, u32[]{:S(2)}) collective-permute-start(f32[6,2048]{1,0:T(8,128)} %own_ref.1), channel_id=1, source_target_pairs={{0,16},{16,0},{1,17},{17,1},{2,18},{18,2},{3,19},{19,3},{4,20},{20... | collective-permute-start | bytes 147464 | tf_op jit(solution)/shard_map/ppermute | solution.py:116
  1.2 1.1 %collective-permute-done.refs_0_ = f32[6,2048]{1,0:T(8,128)S(1)} collective-permute-done((f32[6,2048]{1,0:T(8,128)}, f32[6,2048]{1,0:T(8,128)S(1)}, u32[]{:S(2)}, u32[]{:S(2)}) %collective-permute-start) | collective-permute-done | bytes 49184 | tf_op jit(solution)/shard_map/ppermute | solution.py:116
  2.3 0.0 copy-start
  2.3 0.6 %copy-done = f32[6,2048]{1,0:T(8,128)} copy-done((f32[6,2048]{1,0:T(8,128)}, f32[6,2048]{1,0:T(8,128)S(1)}, u32[]{:S(2)}) %copy-start) | copy-done | bytes 49176
  2.9 5.5 %gram.1 = f32[16,24,96]{2,1,0:T(8,128)} custom-call(f32[6,2048]{1,0:T(8,128)} %own_ref.1, f32[6,2048]{1,0:T(8,128)} %copy-done, s32[1]{0:T(128)} %bitcast.refs_1_, s32[1,2048]{1,0:T(1,128)} %bitcast.3, s32[8,2048]{1,0:T(8,128)} %refs_3_.1, f32[8,2048]{1,0:T(8,128)} %refs_4_.1), custom_call_target="tpu_custom_call" | custom-call | tf_op jit(solution)/shard_map/gram/pallas_call | solution.py:128
  8.4 17.3 %all_to_all.5.parts_ref = f32[16,24,96]{2,1,0:T(8,128)} all-to-all(f32[16,24,96]{2,1,0:T(8,128)} %gram.1), channel_id=1, replica_groups=mesh['grp'=2,'blk'=16] {'blk'}, dimensions={0} | all-to-all | bytes 294912 | tf_op jit(solution)/shard_map/all_to_all | solution.py:135
  25.7 1.6 %factor.1 = (f32[21,96]{1,0:T(8,128)}, f32[1,96]{1,0:T(1,128)}) custom-call(f32[16,24,96]{2,1,0:T(8,128)} %all_to_all.5.parts_ref), custom_call_target="tpu_custom_call" | custom-call | tf_op jit(solution)/shard_map/factor/pallas_call | solution.py:136
Async XLA Ops:
  0.6 1.7 %collective-permute-start = (f32[6,2048]{1,0:T(8,128)}, f32[6,2048]{1,0:T(8,128)S(1)}, u32[]{:S(2)}, u32[]{:S(2)}) collective-permute-start(f32[6,2048]{1,0:T(8,128)} %own_ref.1), channel_id=1, source_target_pairs={{0,16},{16,0},{1,17},{17,1},{2,18},{18,2},{3,19},{19,3},{4,20},{20... | collective-permute-start | bytes 147464 | tf_op jit(solution)/shard_map/ppermute | solution.py:116
  2.3 0.6 %copy-start = (f32[6,2048]{1,0:T(8,128)}, f32[6,2048]{1,0:T(8,128)S(1)}, u32[]{:S(2)}) copy-start(f32[6,2048]{1,0:T(8,128)S(1)} %collective-permute-done.refs_0_) | copy-start | bytes 147460

commit v2 on v1

--- a/solution.py
+++ b/solution.py
@@ -10,6 +10,11 @@
 ROWS_DEV = 2048
 AGG_DEV = 96
 LANES = 128
+NULL_MOST = 6.0
+SPLIT = 11
+SCALE_WHOLE = (2.0 ** (31 - SPLIT) - 1.0) / NULL_MOST
+SCALE_SPLIT = (2.0 ** (2 * SPLIT - 1) - 1.0) / NULL_MOST
+KEEP = (1 << SPLIT) - 1
 
 
 def pair_list(vectors):
@@ -24,37 +29,87 @@
     return lax.shift_right_logical(ids * factor, shift)
 
 
-def gram_kernel(shares, own_ref, *refs):
-    *others, ids_ref, index_ref, weight_ref, out_ref = refs
+def encode(table):
+    words = 2 * table.shape[0] // 3
+    whole = jnp.round(table[:words] * SCALE_WHOLE).astype(jnp.int32)
+    split = jnp.round(table[words:] * SCALE_SPLIT).astype(jnp.int32)
+    lower = [
+        jnp.bitwise_and(split[r // 2 : r // 2 + 1] >> (0 if r % 2 else SPLIT), KEEP) for r in range(words)
+    ]
+    return jnp.bitwise_or(whole << SPLIT, jnp.concatenate(lower, axis=0))
+
+
+def decode(words):
+    values = [(word >> SPLIT).astype(jnp.float32) for word in words]
+    for upper, lower in zip(words[0::2], words[1::2]):
+        split = jnp.bitwise_or((upper << (32 - SPLIT)) >> (32 - 2 * SPLIT), jnp.bitwise_and(lower, KEEP))
+        values.append(split.astype(jnp.float32))
+    return values
+
+
+def pick(picked, index, tables):
+    low = jnp.bitwise_and(index, LANES - 1)
+    for table_ref, base in tables:
+        high = lax.shift_right_arithmetic(index - base, LANES.bit_length() - 1)
+        for chunk in range(table_ref.shape[1] // LANES):
+            found = high == chunk
+            for word in range(len(picked)):
+                row = table_ref[word : word + 1, chunk * LANES : (chunk + 1) * LANES]
+                value = jnp.take_along_axis(
+                    jnp.broadcast_to(row, index.shape), low, axis=1, mode="promise_in_bounds"
+                )
+                picked[word] = jnp.where(found, value, picked[word])
+    return picked
+
+
+def own_kernel(*refs):
+    arguments, copies = refs[:4], refs[4:8]
+    picked_ref, table_ref, sems = refs[8:]
+    rows = copies[0].shape[1]
+    moves = [
+        pltpu.make_async_copy(source, target, sems.at[i])
+        for i, (source, target) in enumerate(zip(arguments, copies))
+    ]
+    for move in moves:
+        move.start()
+    own_ref, index_ref = copies[:2]
+    moves[0].wait()
+    table_ref[...] = encode(own_ref[...])
+    moves[1].wait()
+    for start in range(0, rows, LANES):
+        here = slice(start, start + LANES)
+        index = index_ref[:, here]
+        zero = [jnp.zeros(index.shape, jnp.int32) for _ in range(table_ref.shape[0])]
+        for word, value in enumerate(pick(zero, index, [(table_ref, rows)])):
+            picked_ref[word, :, here] = value
+    moves[2].wait()
+    moves[3].wait()
+
+
+def gram_kernel(shares, count, *refs):
+    own_ref, index_ref, weight_ref, ids_ref, picked_ref = refs[:5]
+    others, starts = refs[5 : 5 + count], refs[5 + count : 5 + 2 * count]
+    out_ref, *table_refs = refs[5 + 2 * count :]
     vectors, rows = own_ref.shape
     pairs = pair_list(vectors)
     padded = out_ref.shape[1]
-    tables = [(own_ref, rows)]
-    for table_ref, start_ref in zip(others[0::2], others[1::2]):
+    tables = []
+    for other_ref, start_ref, table_ref in zip(others, starts, table_refs):
+        table_ref[...] = encode(other_ref[...])
         tables.append((table_ref, start_ref[0]))
+    words = picked_ref.shape[0]
+    scales = [1.0 / SCALE_WHOLE] * words + [1.0 / SCALE_SPLIT] * (vectors - words)
     gram = [jnp.zeros((shares * padded, AGG_DEV), jnp.float32) for _ in range(2)]
     step = 2 * LANES
     for first in range(0, rows, step):
         pieces = []
         for start in range(first, first + step, LANES):
             here = slice(start, start + LANES)
-            index = index_ref[:, here]
             weight = weight_ref[:, here]
-            low = jnp.bitwise_and(index, LANES - 1)
-            picked = [jnp.zeros(index.shape, jnp.float32) for _ in range(vectors)]
-            for table_ref, base in tables:
-                high = lax.shift_right_arithmetic(index - base, 7)
-                for chunk in range(rows // LANES):
-                    found = high == chunk
-                    for v in range(vectors):
-                        row = table_ref[v : v + 1, chunk * LANES : (chunk + 1) * LANES]
-                        value = jnp.take_along_axis(
-                            jnp.broadcast_to(row, index.shape), low, axis=1, mode="promise_in_bounds"
-                        )
-                        picked[v] = jnp.where(found, value, picked[v])
+            picked = pick([picked_ref[word, :, here] for word in range(words)], index_ref[:, here], tables)
             smooth = [
-                own_ref[v : v + 1, here] - jnp.sum(weight * picked[v], axis=0, keepdims=True)
-                for v in range(vectors)
+                own_ref[v : v + 1, here] - jnp.sum(weight * value, axis=0, keepdims=True) * scales[v]
+                for v, value in enumerate(decode(picked))
             ]
             pieces.append([smooth[p] * smooth[q] for p, q in pairs])
         zero = jnp.zeros((padded - len(pairs), step), jnp.float32)
@@ -107,31 +162,44 @@
 
 def shards(nullspace, agg_ids, nbr_index, nbr_weight):
     vectors, rows = nullspace.shape
+    assert vectors % 3 == 0 and rows % (2 * LANES) == 0
+    words = 2 * vectors // 3
     groups, shares = lax.axis_size("grp"), lax.axis_size("blk")
     pairs = pair_list(vectors)
     padded = -(-len(pairs) // 8) * 8
     vmem = pl.BlockSpec(memory_space=pltpu.VMEM)
     smem = pl.BlockSpec(memory_space=pltpu.SMEM)
+    hbm = pl.BlockSpec(memory_space=pltpu.HBM)
     if groups == 2:
-        other = lax.ppermute(nullspace, "grp", [(0, 1), (1, 0)])
-        start = (2 * rows * (1 - lax.axis_index("grp"))).astype(jnp.int32).reshape(1)
-        tables = [other, start]
+        others = [lax.ppermute(nullspace, "grp", [(0, 1), (1, 0)])]
+        starts = [(2 * rows * (1 - lax.axis_index("grp"))).astype(jnp.int32).reshape(1)]
     else:
-        before = lax.ppermute(nullspace, "grp", [(i, i + 1) for i in range(groups - 1)])
-        after = lax.ppermute(nullspace, "grp", [(i + 1, i) for i in range(groups - 1)])
-        tables = [
-            before,
-            jnp.zeros((1,), jnp.int32),
-            after,
-            jnp.full((1,), 2 * rows, jnp.int32),
+        others = [
+            lax.ppermute(nullspace, "grp", [(i, i + 1) for i in range(groups - 1)]),
+            lax.ppermute(nullspace, "grp", [(i + 1, i) for i in range(groups - 1)]),
         ]
+        starts = [jnp.zeros((1,), jnp.int32), jnp.full((1,), 2 * rows, jnp.int32)]
+    arguments = (nullspace, nbr_index, nbr_weight, agg_ids.reshape(1, rows))
+    held = pl.pallas_call(
+        own_kernel,
+        out_shape=[jax.ShapeDtypeStruct(a.shape, a.dtype) for a in arguments]
+        + [jax.ShapeDtypeStruct((words,) + nbr_index.shape, jnp.int32)],
+        in_specs=[hbm] * 4,
+        out_specs=[vmem] * 5,
+        scratch_shapes=[pltpu.VMEM((words, rows), jnp.int32), pltpu.SemaphoreType.DMA((4,))],
+        compiler_params=pltpu.CompilerParams(vmem_limit_bytes=4 << 20),
+        cost_estimate=pl.CostEstimate(flops=1 << 22, bytes_accessed=1 << 18, transcendentals=0),
+        name="own",
+    )(*[pltpu.with_memory_space_constraint(a, pltpu.HBM) for a in arguments])
     partial = pl.pallas_call(
-        functools.partial(gram_kernel, shares),
+        functools.partial(gram_kernel, shares, len(others)),
         out_shape=jax.ShapeDtypeStruct((shares, padded, AGG_DEV), jnp.float32),
-        in_specs=[vmem] + [vmem, smem] * (len(tables) // 2) + [vmem] * 3,
+        in_specs=[vmem] * (5 + len(others)) + [smem] * len(others),
         out_specs=vmem,
+        scratch_shapes=[pltpu.VMEM((words, rows), jnp.int32) for _ in others],
+        compiler_params=pltpu.CompilerParams(vmem_limit_bytes=8 << 20),
         name="gram",
-    )(nullspace, *tables, agg_ids.reshape(1, rows), nbr_index, nbr_weight)
+    )(*held, *others, *starts)
     parts = lax.all_to_all(partial, "blk", 0, 0, tiled=True)
     factor, spread = pl.pallas_call(
         functools.partial(factor_kernel, vectors),
@@ -141,6 +209,7 @@
         ),
         in_specs=[vmem],
         out_specs=(vmem, vmem),
+        compiler_params=pltpu.CompilerParams(vmem_limit_bytes=4 << 20),
         name="factor",
     )(parts)
     return factor, spread.reshape(AGG_DEV)

time: 27.6 us -> 22.9 us (0.83)
  Pallas kernels: 7.13 us -> 4.82 us
  waiting for transfers between devices: 1.11 us -> 0.01 us
  blocking collectives: 17.3 us -> 16.6 us
  local copies, waits for them, and re-layouts: 0.62 us -> 0 us
    pallas_call x1 -> x2, Pallas kernels: 5.48 us -> 4.09 us  [the longest x1 2.11 us: shards(): pl.pallas_call(own_kernel, out_shape=[jax.ShapeDtypeStruct(a.shape, a.dty...]
    ppermute x1, waiting for transfers between devices: 1.11 us -> 0.01 us  [shards(): others = [lax.ppermute(nullspace, 'grp', [(0, 1), (1, 0)])]]
    pallas_call x1, Pallas kernels: 1.65 us -> 0.72 us  [shards(): pl.pallas_call(functools.partial(factor_kernel, vectors), out_shape=(jax....]
    all_to_all x1, blocking collectives: 17.3 us -> 16.6 us  [shards(): parts = lax.all_to_all(partial, 'blk', 0, 0, tiled=True)]
    unnamed x2 -> x0, local copies, waits for them, and re-layouts: 0.62 us -> none
  transfers between devices with their start and end apart: 1 -> 1, of which waited for: 1 -> 0; matrix products, arithmetic and copies ran while one was open for 0% -> 0% of each run, Pallas kernels for 0% -> 9%
where the time goes in v2:
time: 22.9 us; the launch traced here: 22.7 us
  blocking collectives  16.6 us (72%)
  Pallas kernels  4.82 us (21%)
  between operations  0.65 us (3%)
  starting transfers between devices  0.56 us (2%)
    all_to_all x1, blocking collectives, shards(): parts = lax.all_to_all(partial, 'blk', 0, 0, tiled=True)  16.6 us
    pallas_call x1, Pallas kernels, shards(): pl.pallas_call(own_kernel, out_shape=[jax.ShapeDtypeStruct(a.shape, a.dty...  2.11 us
    pallas_call x1, Pallas kernels, shards(): pl.pallas_call(functools.partial(gram_kernel, shares, len(others)), out_s...  1.98 us
    pallas_call x1, Pallas kernels, shards(): pl.pallas_call(functools.partial(factor_kernel, vectors), out_shape=(jax....  0.72 us
    ppermute x1, starting transfers between devices, shards(): others = [lax.ppermute(nullspace, 'grp', [(0, 1), (1, 0)])]  0.56 us
  transfers between devices with their start and end apart: 1, of which 0 were waited for; matrix products, arithmetic and copies ran while one was open for 0% of the time, Pallas kernels for 9%

profile of v2, /device:TPU:0, one launch (start us, length us, event | category | flops | bytes accessed | tf_op | source)
XLA Modules:
  0.0 22.7 jit_solution(2820769496072990426)
XLA Ops:
  0.6 0.6 %collective-permute-start = (f32[6,2048]{1,0:T(8,128)}, f32[6,2048]{1,0:T(8,128)S(1)}, u32[]{:S(2)}, u32[]{:S(2)}) collective-permute-start(f32[6,2048]{1,0:T(8,128)} %refs_0_.1), channel_id=1, source_target_pairs={{0,16},{16,0},{1,17},{17,1},{2,18},{18,2},{3,19},{19,3},{4,20},{20... | collective-permute-start | bytes 147464 | tf_op jit(solution)/shard_map/ppermute | solution.py:174
  1.2 2.1 %own.1 = (f32[6,2048]{1,0:T(8,128)S(1)}, s32[8,2048]{1,0:T(8,128)S(1)}, f32[8,2048]{1,0:T(8,128)S(1)}, s32[1,2048]{1,0:T(1,128)S(1)}, s32[4,8,2048]{2,1,0:T(8,128)S(1)}) custom-call(f32[6,2048]{1,0:T(8,128)} %refs_0_.1, s32[8,2048]{1,0:T(8,128)} %refs_1_.1, f32[8,2048]{1,0:T(8,128)} %refs_2_.1, s32[1,2048]{1,0:T(1,128)} %bitcast.3), custom_call_target="tpu_custom_call" | custom-call | flops 4194304 | bytes 262144 | tf_op jit(solution)/shard_map/own/pallas_call | solution.py:183
  3.3 0.0 collective-permute-done.refs_5_
  3.3 2.0 %gram.1 = f32[16,24,96]{2,1,0:T(8,128)S(1)} custom-call(f32[6,2048]{1,0:T(8,128)S(1)} %get-tuple-element.9.refs_0_, s32[8,2048]{1,0:T(8,128)S(1)} %get-tuple-element.10.refs_1_, f32[8,2048]{1,0:T(8,128)S(1)} %get-tuple-element.11.refs_2_, s32[1,2048]{1,0:T(1,128)S(1)} %get-tuple-element.12.refs_3_, s32[4,8,2048]{2,1,0:T(8,128)S(1)} %get-tuple-element.13.refs_4_, ...), custom_call_target="tpu_custom_call" | custom-call | tf_op jit(solution)/shard_map/gram/pallas_call | solution.py:194
  5.3 16.6 %all_to_all.5.parts_ref = f32[16,24,96]{2,1,0:T(8,128)S(1)} all-to-all(f32[16,24,96]{2,1,0:T(8,128)S(1)} %gram.1), channel_id=1, replica_groups=mesh['grp'=2,'blk'=16] {'blk'}, dimensions={0} | all-to-all | bytes 294912 | tf_op jit(solution)/shard_map/all_to_all | solution.py:203
  21.9 0.7 %factor.1 = (f32[21,96]{1,0:T(8,128)}, f32[1,96]{1,0:T(1,128)}) custom-call(f32[16,24,96]{2,1,0:T(8,128)S(1)} %all_to_all.5.parts_ref), custom_call_target="tpu_custom_call" | custom-call | tf_op jit(solution)/shard_map/factor/pallas_call | solution.py:204
Async XLA Ops:
  0.6 2.7 %collective-permute-start = (f32[6,2048]{1,0:T(8,128)}, f32[6,2048]{1,0:T(8,128)S(1)}, u32[]{:S(2)}, u32[]{:S(2)}) collective-permute-start(f32[6,2048]{1,0:T(8,128)} %refs_0_.1), channel_id=1, source_target_pairs={{0,16},{16,0},{1,17},{17,1},{2,18},{18,2},{3,19},{19,3},{4,20},{20... | collective-permute-start | bytes 147464 | tf_op jit(solution)/shard_map/ppermute | solution.py:174

commit v3 on v2

--- a/solution.py
+++ b/solution.py
@@ -47,6 +47,22 @@
     return values
 
 
+def lane_pick(rows, low):
+    return lax.gather(
+        rows,
+        low[:, :, None],
+        lax.GatherDimensionNumbers(
+            offset_dims=(),
+            collapsed_slice_dims=(1,),
+            start_index_map=(1,),
+            operand_batching_dims=(0,),
+            start_indices_batching_dims=(0,),
+        ),
+        slice_sizes=(1, 1),
+        mode=lax.GatherScatterMode.PROMISE_IN_BOUNDS,
+    )
+
+
 def pick(picked, index, tables):
     low = jnp.bitwise_and(index, LANES - 1)
     for table_ref, base in tables:
@@ -55,16 +71,14 @@
             found = high == chunk
             for word in range(len(picked)):
                 row = table_ref[word : word + 1, chunk * LANES : (chunk + 1) * LANES]
-                value = jnp.take_along_axis(
-                    jnp.broadcast_to(row, index.shape), low, axis=1, mode="promise_in_bounds"
-                )
+                value = lane_pick(jnp.broadcast_to(row, index.shape), low)
                 picked[word] = jnp.where(found, value, picked[word])
     return picked
 
 
-def own_kernel(*refs):
+def own_kernel(shares, *refs):
     arguments, copies = refs[:4], refs[4:8]
-    picked_ref, table_ref, sems = refs[8:]
+    picked_ref, column_ref, table_ref, sems = refs[8:]
     rows = copies[0].shape[1]
     moves = [
         pltpu.make_async_copy(source, target, sems.at[i])
@@ -72,10 +86,11 @@
     ]
     for move in moves:
         move.start()
-    own_ref, index_ref = copies[:2]
+    own_ref, index_ref, _, ids_ref = copies
     moves[0].wait()
     table_ref[...] = encode(own_ref[...])
     moves[1].wait()
+    moves[3].wait()
     for start in range(0, rows, LANES):
         here = slice(start, start + LANES)
         index = index_ref[:, here]
@@ -83,24 +98,52 @@
         for word, value in enumerate(pick(zero, index, [(table_ref, rows)])):
             picked_ref[word, :, here] = value
     moves[2].wait()
-    moves[3].wait()
+
+
+def to_wire(gram):
+    tail = jnp.concatenate([gram[16:], jnp.zeros((8, LANES - AGG_DEV), gram.dtype)], axis=1)
+    lanes = lax.broadcasted_iota(jnp.int32, (8, LANES), 1)
+    rows = lax.broadcasted_iota(jnp.int32, (8, LANES), 0)
+    out = []
+    third = AGG_DEV // 3
+    thirds = [pltpu.roll(tail, AGG_DEV - third * i, 1) for i in range(3)]
+    for half in range(2):
+        main = jnp.concatenate(
+            [gram[8 * half : 8 * half + 8], jnp.zeros((8, LANES - AGG_DEV), gram.dtype)], axis=1
+        )
+        last = pltpu.roll(thirds[2], 5 - 3 * half, 0)
+        side = jnp.where(rows < 5, thirds[half], last)
+        out.append(jnp.where(lanes < AGG_DEV, main, side))
+    return jnp.concatenate(out, axis=0)
+
+
+def from_wire(wire):
+    third = AGG_DEV // 3
+    lanes = lax.broadcasted_iota(jnp.int32, (8, LANES), 1)
+    rows = lax.broadcasted_iota(jnp.int32, (8, LANES), 0)
+    first, second = wire[:8], wire[8:]
+    last = jnp.where(rows < 3, pltpu.roll(first, 3, 0), pltpu.roll(second, 6, 0))
+    thirds = [pltpu.roll(x, LANES - AGG_DEV + third * i, 1) for i, x in enumerate((first, second, last))]
+    tail = jnp.where(lanes < third, thirds[0], jnp.where(lanes < 2 * third, thirds[1], thirds[2]))
+    return jnp.concatenate([first, second, tail], axis=0)
 
 
 def gram_kernel(shares, count, *refs):
-    own_ref, index_ref, weight_ref, ids_ref, picked_ref = refs[:5]
-    others, starts = refs[5 : 5 + count], refs[5 + count : 5 + 2 * count]
-    out_ref, *table_refs = refs[5 + 2 * count :]
+    own_ref, index_ref, weight_ref, ids_ref, picked_ref, column_ref = refs[:6]
+    others, starts = refs[6 : 6 + count], refs[6 + count : 6 + 2 * count]
+    out_ref, *table_refs = refs[6 + 2 * count :]
     vectors, rows = own_ref.shape
     pairs = pair_list(vectors)
-    padded = out_ref.shape[1]
+    padded = 24
     tables = []
     for other_ref, start_ref, table_ref in zip(others, starts, table_refs):
         table_ref[...] = encode(other_ref[...])
         tables.append((table_ref, start_ref[0]))
     words = picked_ref.shape[0]
     scales = [1.0 / SCALE_WHOLE] * words + [1.0 / SCALE_SPLIT] * (vectors - words)
-    gram = [jnp.zeros((shares * padded, AGG_DEV), jnp.float32) for _ in range(2)]
-    step = 2 * LANES
+    half_shares = shares // 2
+    gram = [jnp.zeros((half_shares * 2 * padded, AGG_DEV), jnp.float32) for _ in range(2)]
+    step = LANES
     for first in range(0, rows, step):
         pieces = []
         for start in range(first, first + step, LANES):
@@ -118,19 +161,28 @@
             axis=0,
         )
         coarse = terms.astype(jnp.bfloat16).astype(jnp.float32)
+        both = jnp.concatenate([coarse, terms - coarse], axis=0)
+        share = share_of(ids_ref[:, first : first + step], shares)
         ids = ids_ref[:, first : first + step]
-        share = share_of(ids, shares)
         within = ids - share * AGG_DEV
-        lanes = lax.broadcasted_iota(jnp.int32, (AGG_DEV, step), 0)
-        one_hot = (lanes == within).astype(jnp.float32).astype(jnp.bfloat16)
-        for piece, part in enumerate((coarse, terms - coarse)):
-            spread_out = jnp.concatenate(
-                [jnp.where(share == s, part, 0.0) for s in range(shares)], axis=0
+        columns = lax.broadcasted_iota(jnp.int32, (AGG_DEV, step), 0)
+        one_hot = (columns == within).astype(jnp.float32).astype(jnp.bfloat16)
+        for half in range(2):
+            masked = jnp.concatenate(
+                [jnp.where(share == half * half_shares + s, both, 0.0) for s in range(half_shares)], axis=0
             ).astype(jnp.bfloat16)
-            gram[piece] = gram[piece] + lax.dot_general(
-                spread_out, one_hot, (((1,), (1,)), ((), ())), preferred_element_type=jnp.float32
+            gram[half] = gram[half] + lax.dot_general(
+                masked,
+                one_hot,
+                (((1,), (1,)), ((), ())),
+                preferred_element_type=jnp.float32,
             )
-    out_ref[...] = (gram[0] + gram[1]).reshape(out_ref.shape)
+    for half in range(2):
+        for s in range(half_shares):
+            at = 2 * padded * s
+            out_ref[half * half_shares + s] = to_wire(
+                gram[half][at : at + padded] + gram[half][at + padded : at + 2 * padded]
+            )
 
 
 def factor_kernel(vectors, parts_ref, factor_ref, spread_ref):
@@ -138,6 +190,7 @@
     total = parts_ref[0]
     for source in range(1, parts_ref.shape[0]):
         total = total + parts_ref[source]
+    total = from_wire(total)[:, :AGG_DEV]
     entry = {}
     for i, (p, q) in enumerate(pairs):
         value = total[i : i + 1] * (AGG_DEV / ROWS_DEV)
@@ -166,7 +219,7 @@
     words = 2 * vectors // 3
     groups, shares = lax.axis_size("grp"), lax.axis_size("blk")
     pairs = pair_list(vectors)
-    padded = -(-len(pairs) // 8) * 8
+    assert len(pairs) == 21 and shares % 2 == 0
     vmem = pl.BlockSpec(memory_space=pltpu.VMEM)
     smem = pl.BlockSpec(memory_space=pltpu.SMEM)
     hbm = pl.BlockSpec(memory_space=pltpu.HBM)
@@ -181,11 +234,14 @@
         starts = [jnp.zeros((1,), jnp.int32), jnp.full((1,), 2 * rows, jnp.int32)]
     arguments = (nullspace, nbr_index, nbr_weight, agg_ids.reshape(1, rows))
     held = pl.pallas_call(
-        own_kernel,
+        functools.partial(own_kernel, shares),
         out_shape=[jax.ShapeDtypeStruct(a.shape, a.dtype) for a in arguments]
-        + [jax.ShapeDtypeStruct((words,) + nbr_index.shape, jnp.int32)],
+        + [
+            jax.ShapeDtypeStruct((words,) + nbr_index.shape, jnp.int32),
+            jax.ShapeDtypeStruct((AGG_DEV, rows), jnp.bfloat16),
+        ],
         in_specs=[hbm] * 4,
-        out_specs=[vmem] * 5,
+        out_specs=[vmem] * 6,
         scratch_shapes=[pltpu.VMEM((words, rows), jnp.int32), pltpu.SemaphoreType.DMA((4,))],
         compiler_params=pltpu.CompilerParams(vmem_limit_bytes=4 << 20),
         cost_estimate=pl.CostEstimate(flops=1 << 22, bytes_accessed=1 << 18, transcendentals=0),
@@ -193,8 +249,8 @@
     )(*[pltpu.with_memory_space_constraint(a, pltpu.HBM) for a in arguments])
     partial = pl.pallas_call(
         functools.partial(gram_kernel, shares, len(others)),
-        out_shape=jax.ShapeDtypeStruct((shares, padded, AGG_DEV), jnp.float32),
-        in_specs=[vmem] * (5 + len(others)) + [smem] * len(others),
+        out_shape=jax.ShapeDtypeStruct((shares, 16, LANES), jnp.float32),
+        in_specs=[vmem] * (6 + len(others)) + [smem] * len(others),
         out_specs=vmem,
         scratch_shapes=[pltpu.VMEM((words, rows), jnp.int32) for _ in others],
         compiler_params=pltpu.CompilerParams(vmem_limit_bytes=8 << 20),

time: 22.9 us -> 21.8 us (0.952)
  blocking collectives: 16.6 us -> 15.8 us
    all_to_all x1, blocking collectives: 16.6 us -> 15.8 us  [shards(): parts = lax.all_to_all(partial, 'blk', 0, 0, tiled=True)]
  transfers between devices with their start and end apart: 1 -> 1, of which waited for: 0 -> 0; matrix products, arithmetic and copies ran while one was open for 0% -> 0% of each run, Pallas kernels for 9% -> 10%
where the time goes in v3:
time: 21.8 us; the launch traced here: 21.6 us
  blocking collectives  15.8 us (72%)
  Pallas kernels  4.6 us (21%)
  between operations  0.66 us (3%)
  starting transfers between devices  0.56 us (3%)
    all_to_all x1, blocking collectives, shards(): parts = lax.all_to_all(partial, 'blk', 0, 0, tiled=True)  15.8 us
    pallas_call x1, Pallas kernels, shards(): pl.pallas_call(functools.partial(own_kernel, shares), out_shape=[jax.Shap...  2.11 us
    pallas_call x1, Pallas kernels, shards(): pl.pallas_call(functools.partial(gram_kernel, shares, len(others)), out_s...  1.77 us
    pallas_call x1, Pallas kernels, shards(): pl.pallas_call(functools.partial(factor_kernel, vectors), out_shape=(jax....  0.72 us
    ppermute x1, starting transfers between devices, shards(): others = [lax.ppermute(nullspace, 'grp', [(0, 1), (1, 0)])]  0.56 us
  transfers between devices with their start and end apart: 1, of which 0 were waited for; matrix products, arithmetic and copies ran while one was open for 0% of the time, Pallas kernels for 10%

profile of v3, /device:TPU:0, one launch (start us, length us, event | category | flops | bytes accessed | tf_op | source)
XLA Modules:
  0.0 21.6 jit_solution(4529908244041837756)
XLA Ops:
  0.6 0.6 %collective-permute-start = (f32[6,2048]{1,0:T(8,128)}, f32[6,2048]{1,0:T(8,128)S(1)}, u32[]{:S(2)}, u32[]{:S(2)}) collective-permute-start(f32[6,2048]{1,0:T(8,128)} %refs_0_.1), channel_id=1, source_target_pairs={{0,16},{16,0},{1,17},{17,1},{2,18},{18,2},{3,19},{19,3},{4,20},{20... | collective-permute-start | bytes 147464 | tf_op jit(solution)/shard_map/ppermute | solution.py:227
  1.2 2.1 %own.1 = (f32[6,2048]{1,0:T(8,128)S(1)}, s32[8,2048]{1,0:T(8,128)S(1)}, f32[8,2048]{1,0:T(8,128)S(1)}, s32[1,2048]{1,0:T(1,128)S(1)}, s32[4,8,2048]{2,1,0:T(8,128)S(1)}, /*index=5*/bf16[96,2048]{1,0:T(8,128)(2,1)S(1)}) custom-call(f32[6,2048]{1,0:T(8,128)} %refs_0_.1, s32[8,2048]{1,0:T(8,128)} %refs_1_.1, f32[8,2048]{1,0:T(8,128)} %refs_2_.1, s32[1,2048]{1,0:T(1,128)} %bitcast.3), custom_call_target="tpu_custom_call" | custom-call | flops 4194304 | bytes 262144 | tf_op jit(solution)/shard_map/own/pallas_call | solution.py:236
  3.3 0.0 collective-permute-done.refs_6_
  3.3 1.8 %gram.1 = f32[16,16,128]{2,1,0:T(8,128)S(1)} custom-call(f32[6,2048]{1,0:T(8,128)S(1)} %get-tuple-element.10.refs_0_, s32[8,2048]{1,0:T(8,128)S(1)} %get-tuple-element.11.refs_1_, f32[8,2048]{1,0:T(8,128)S(1)} %get-tuple-element.12.refs_2_, s32[1,2048]{1,0:T(1,128)S(1)} %get-tuple-element.13.refs_3_, s32[4,8,2048]{2,1,0:T(8,128)S(1)} %get-tuple-element.14.refs_4_, ...), custom_call_target="tpu_custom_call" | custom-call | tf_op jit(solution)/shard_map/gram/pallas_call | solution.py:250
  5.1 15.8 %all_to_all.5.parts_ref = f32[16,16,128]{2,1,0:T(8,128)S(1)} all-to-all(f32[16,16,128]{2,1,0:T(8,128)S(1)} %gram.1), channel_id=1, replica_groups=mesh['grp'=2,'blk'=16] {'blk'}, dimensions={0} | all-to-all | bytes 262144 | tf_op jit(solution)/shard_map/all_to_all | solution.py:259
  20.8 0.7 %factor.1 = (f32[21,96]{1,0:T(8,128)}, f32[1,96]{1,0:T(1,128)}) custom-call(f32[16,16,128]{2,1,0:T(8,128)S(1)} %all_to_all.5.parts_ref), custom_call_target="tpu_custom_call" | custom-call | tf_op jit(solution)/shard_map/factor/pallas_call | solution.py:260
Async XLA Ops:
  0.6 2.7 %collective-permute-start = (f32[6,2048]{1,0:T(8,128)}, f32[6,2048]{1,0:T(8,128)S(1)}, u32[]{:S(2)}, u32[]{:S(2)}) collective-permute-start(f32[6,2048]{1,0:T(8,128)} %refs_0_.1), channel_id=1, source_target_pairs={{0,16},{16,0},{1,17},{17,1},{2,18},{18,2},{3,19},{19,3},{4,20},{20... | collective-permute-start | bytes 147464 | tf_op jit(solution)/shard_map/ppermute | solution.py:227

commit v4 on v3

--- a/solution.py
+++ b/solution.py
@@ -15,6 +15,7 @@
 SCALE_WHOLE = (2.0 ** (31 - SPLIT) - 1.0) / NULL_MOST
 SCALE_SPLIT = (2.0 ** (2 * SPLIT - 1) - 1.0) / NULL_MOST
 KEEP = (1 << SPLIT) - 1
+PARITY_STEPS = 30
 
 
 def pair_list(vectors):
@@ -76,28 +77,23 @@
     return picked
 
 
-def own_kernel(shares, *refs):
-    arguments, copies = refs[:4], refs[4:8]
-    picked_ref, column_ref, table_ref, sems = refs[8:]
-    rows = copies[0].shape[1]
+def own_kernel(own_ref, index_ref, weight_hbm, ids_hbm, weight_ref, ids_ref, picked_ref, table_ref, sems):
+    rows = own_ref.shape[1]
     moves = [
-        pltpu.make_async_copy(source, target, sems.at[i])
-        for i, (source, target) in enumerate(zip(arguments, copies))
+        pltpu.make_async_copy(weight_hbm, weight_ref, sems.at[0]),
+        pltpu.make_async_copy(ids_hbm, ids_ref, sems.at[1]),
     ]
     for move in moves:
         move.start()
-    own_ref, index_ref, _, ids_ref = copies
-    moves[0].wait()
     table_ref[...] = encode(own_ref[...])
-    moves[1].wait()
-    moves[3].wait()
     for start in range(0, rows, LANES):
         here = slice(start, start + LANES)
         index = index_ref[:, here]
         zero = [jnp.zeros(index.shape, jnp.int32) for _ in range(table_ref.shape[0])]
         for word, value in enumerate(pick(zero, index, [(table_ref, rows)])):
             picked_ref[word, :, here] = value
-    moves[2].wait()
+    for move in moves:
+        move.wait()
 
 
 def to_wire(gram):
@@ -129,9 +125,9 @@
 
 
 def gram_kernel(shares, count, *refs):
-    own_ref, index_ref, weight_ref, ids_ref, picked_ref, column_ref = refs[:6]
-    others, starts = refs[6 : 6 + count], refs[6 + count : 6 + 2 * count]
-    out_ref, *table_refs = refs[6 + 2 * count :]
+    own_ref, index_ref, weight_ref, ids_ref, picked_ref = refs[:5]
+    others, starts = refs[5 : 5 + count], refs[5 + count : 5 + 2 * count]
+    out_ref, *table_refs = refs[5 + 2 * count :]
     vectors, rows = own_ref.shape
     pairs = pair_list(vectors)
     padded = 24
@@ -225,37 +221,46 @@
     hbm = pl.BlockSpec(memory_space=pltpu.HBM)
     if groups == 2:
         others = [lax.ppermute(nullspace, "grp", [(0, 1), (1, 0)])]
-        starts = [(2 * rows * (1 - lax.axis_index("grp"))).astype(jnp.int32).reshape(1)]
+        group = lax.axis_index("grp").astype(jnp.int32)
+        for n in range(PARITY_STEPS):
+            group = group * 3 + 2 * (n + 1)
+        group = jnp.bitwise_and(group, 1)
+        starts = [(2 * rows * (1 - group)).reshape(1)]
     else:
         others = [
             lax.ppermute(nullspace, "grp", [(i, i + 1) for i in range(groups - 1)]),
             lax.ppermute(nullspace, "grp", [(i + 1, i) for i in range(groups - 1)]),
         ]
         starts = [jnp.zeros((1,), jnp.int32), jnp.full((1,), 2 * rows, jnp.int32)]
-    arguments = (nullspace, nbr_index, nbr_weight, agg_ids.reshape(1, rows))
-    held = pl.pallas_call(
-        functools.partial(own_kernel, shares),
-        out_shape=[jax.ShapeDtypeStruct(a.shape, a.dtype) for a in arguments]
-        + [
+    ids = agg_ids.reshape(1, rows)
+    weight, ids, picked = pl.pallas_call(
+        own_kernel,
+        out_shape=[
+            jax.ShapeDtypeStruct(nbr_weight.shape, nbr_weight.dtype),
+            jax.ShapeDtypeStruct(ids.shape, ids.dtype),
             jax.ShapeDtypeStruct((words,) + nbr_index.shape, jnp.int32),
-            jax.ShapeDtypeStruct((AGG_DEV, rows), jnp.bfloat16),
         ],
-        in_specs=[hbm] * 4,
-        out_specs=[vmem] * 6,
-        scratch_shapes=[pltpu.VMEM((words, rows), jnp.int32), pltpu.SemaphoreType.DMA((4,))],
+        in_specs=[vmem, vmem, hbm, hbm],
+        out_specs=[vmem] * 3,
+        scratch_shapes=[pltpu.VMEM((words, rows), jnp.int32), pltpu.SemaphoreType.DMA((2,))],
         compiler_params=pltpu.CompilerParams(vmem_limit_bytes=4 << 20),
         cost_estimate=pl.CostEstimate(flops=1 << 22, bytes_accessed=1 << 18, transcendentals=0),
         name="own",
-    )(*[pltpu.with_memory_space_constraint(a, pltpu.HBM) for a in arguments])
+    )(
+        nullspace,
+        nbr_index,
+        pltpu.with_memory_space_constraint(nbr_weight, pltpu.HBM),
+        pltpu.with_memory_space_constraint(ids, pltpu.HBM),
+    )
     partial = pl.pallas_call(
         functools.partial(gram_kernel, shares, len(others)),
         out_shape=jax.ShapeDtypeStruct((shares, 16, LANES), jnp.float32),
-        in_specs=[vmem] * (6 + len(others)) + [smem] * len(others),
+        in_specs=[vmem] * (5 + len(others)) + [smem] * len(others),
         out_specs=vmem,
         scratch_shapes=[pltpu.VMEM((words, rows), jnp.int32) for _ in others],
         compiler_params=pltpu.CompilerParams(vmem_limit_bytes=8 << 20),
         name="gram",
-    )(*held, *others, *starts)
+    )(nullspace, nbr_index, weight, ids, picked, *others, *starts)
     parts = lax.all_to_all(partial, "blk", 0, 0, tiled=True)
     factor, spread = pl.pallas_call(
         functools.partial(factor_kernel, vectors),

time: 21.8 us -> 21.4 us (0.982)
  Pallas kernels: 4.6 us -> 3.72 us
  local copies, waits for them, and re-layouts: 0 us -> 0.3 us
    pallas_call x1, Pallas kernels: 2.11 us -> 1.24 us  [shards(): pl.pallas_call(own_kernel, out_shape=[jax.ShapeDtypeStruct(nbr_weight.sha...]
    unnamed x0 -> x4, local copies, waits for them, and re-layouts: none -> 0.3 us
  transfers between devices with their start and end apart: 1 -> 1, of which waited for: 0 -> 0; matrix products, arithmetic and copies ran while one was open for 0% -> 0% of each run, Pallas kernels for 10% -> 6%
where the time goes in v4:
time: 21.4 us; the launch traced here: 21.2 us
  blocking collectives  15.9 us (74%)
  Pallas kernels  3.72 us (17%)
  between operations  0.67 us (3%)
  starting transfers between devices  0.56 us (3%)
  local copies, waits for them, and re-layouts  0.3 us (1%)
    all_to_all x1, blocking collectives, shards(): parts = lax.all_to_all(partial, 'blk', 0, 0, tiled=True)  15.9 us
    pallas_call x1, Pallas kernels, shards(): pl.pallas_call(functools.partial(gram_kernel, shares, len(others)), out_s...  1.76 us
    pallas_call x1, Pallas kernels, shards(): pl.pallas_call(own_kernel, out_shape=[jax.ShapeDtypeStruct(nbr_weight.sha...  1.24 us
    pallas_call x1, Pallas kernels, shards(): pl.pallas_call(functools.partial(factor_kernel, vectors), out_shape=(jax....  0.72 us
    ppermute x1, starting transfers between devices, shards(): others = [lax.ppermute(nullspace, 'grp', [(0, 1), (1, 0)])]  0.56 us
  transfers between devices with their start and end apart: 1, of which 0 were waited for; matrix products, arithmetic and copies ran while one was open for 0% of the time, Pallas kernels for 6%

profile of v4, /device:TPU:0, one launch (start us, length us, event | category | flops | bytes accessed | tf_op | source)
XLA Modules:
  0.0 21.2 jit_solution(9620724935016149236)
XLA Ops:
  0.6 0.0 copy-start
  0.6 0.0 copy-start.1
  0.7 0.6 %collective-permute-start = (f32[6,2048]{1,0:T(8,128)}, f32[6,2048]{1,0:T(8,128)S(1)}, u32[]{:S(2)}, u32[]{:S(2)}) collective-permute-start(f32[6,2048]{1,0:T(8,128)} %refs_0_.1), channel_id=1, source_target_pairs={{0,16},{16,0},{1,17},{17,1},{2,18},{18,2},{3,19},{19,3},{4,20},{20... | collective-permute-start | bytes 147464 | tf_op jit(solution)/shard_map/ppermute | solution.py:223
  1.2 0.3 %copy-done = f32[6,2048]{1,0:T(8,128)S(1)} copy-done((f32[6,2048]{1,0:T(8,128)S(1)}, f32[6,2048]{1,0:T(8,128)}, u32[]{:S(2)}) %copy-start) | copy-done | bytes 49176
  1.5 0.0 copy-done.1
  1.5 1.2 %own.1 = (f32[8,2048]{1,0:T(8,128)S(1)}, s32[1,2048]{1,0:T(1,128)S(1)}, s32[4,8,2048]{2,1,0:T(8,128)S(1)}) custom-call(f32[6,2048]{1,0:T(8,128)S(1)} %copy-done, s32[8,2048]{1,0:T(8,128)S(1)} %copy-done.1, f32[8,2048]{1,0:T(8,128)} %weight_hbm.1, s32[1,2048]{1,0:T(1,128)} %bitcast.3), custom_call_target="tpu_custom_call" | custom-call | flops 4194304 | bytes 262144 | tf_op jit(solution)/shard_map/own/pallas_call | solution.py:236
  2.7 0.0 collective-permute-done.refs_5_
  2.8 1.8 %gram.1 = f32[16,16,128]{2,1,0:T(8,128)S(1)} custom-call(f32[6,2048]{1,0:T(8,128)S(1)} %copy-done, s32[8,2048]{1,0:T(8,128)S(1)} %copy-done.1, f32[8,2048]{1,0:T(8,128)S(1)} %get-tuple-element.7.refs_2_, s32[1,2048]{1,0:T(1,128)S(1)} %get-tuple-element.8.refs_3_, s32[4,8,2048]{2,1,0:T(8,128)S(1)} %get-tuple-element.9.refs_4_, ...), custom_call_target="tpu_custom_call" | custom-call | tf_op jit(solution)/shard_map/gram/pallas_call | solution.py:255
  4.5 15.9 %all_to_all.5.parts_ref = f32[16,16,128]{2,1,0:T(8,128)S(1)} all-to-all(f32[16,16,128]{2,1,0:T(8,128)S(1)} %gram.1), channel_id=1, replica_groups=mesh['grp'=2,'blk'=16] {'blk'}, dimensions={0} | all-to-all | bytes 262144 | tf_op jit(solution)/shard_map/all_to_all | solution.py:264
  20.5 0.7 %factor.1 = (f32[21,96]{1,0:T(8,128)}, f32[1,96]{1,0:T(1,128)}) custom-call(f32[16,16,128]{2,1,0:T(8,128)S(1)} %all_to_all.5.parts_ref), custom_call_target="tpu_custom_call" | custom-call | tf_op jit(solution)/shard_map/factor/pallas_call | solution.py:265
Async XLA Ops:
  0.6 0.8 %copy-start = (f32[6,2048]{1,0:T(8,128)S(1)}, f32[6,2048]{1,0:T(8,128)}, u32[]{:S(2)}) copy-start(f32[6,2048]{1,0:T(8,128)} %refs_0_.1) | copy-start | bytes 147460
  0.6 0.9 %copy-start.1 = (s32[8,2048]{1,0:T(8,128)S(1)}, s32[8,2048]{1,0:T(8,128)}, u32[]{:S(2)}) copy-start(s32[8,2048]{1,0:T(8,128)} %refs_1_.1) | copy-start | bytes 196612
  0.7 2.1 %collective-permute-start = (f32[6,2048]{1,0:T(8,128)}, f32[6,2048]{1,0:T(8,128)S(1)}, u32[]{:S(2)}, u32[]{:S(2)}) collective-permute-start(f32[6,2048]{1,0:T(8,128)} %refs_0_.1), channel_id=1, source_target_pairs={{0,16},{16,0},{1,17},{17,1},{2,18},{18,2},{3,19},{19,3},{4,20},{20... | collective-permute-start | bytes 147464 | tf_op jit(solution)/shard_map/ppermute | solution.py:223

commit v5 on v4

--- a/solution.py
+++ b/solution.py
@@ -64,14 +64,14 @@
     )
 
 
-def pick(picked, index, tables):
+def pick(picked, index, tables, first=0):
     low = jnp.bitwise_and(index, LANES - 1)
     for table_ref, base in tables:
         high = lax.shift_right_arithmetic(index - base, LANES.bit_length() - 1)
         for chunk in range(table_ref.shape[1] // LANES):
             found = high == chunk
             for word in range(len(picked)):
-                row = table_ref[word : word + 1, chunk * LANES : (chunk + 1) * LANES]
+                row = table_ref[first + word : first + word + 1, chunk * LANES : (chunk + 1) * LANES]
                 value = lane_pick(jnp.broadcast_to(row, index.shape), low)
                 picked[word] = jnp.where(found, value, picked[word])
     return picked
@@ -89,9 +89,11 @@
     for start in range(0, rows, LANES):
         here = slice(start, start + LANES)
         index = index_ref[:, here]
-        zero = [jnp.zeros(index.shape, jnp.int32) for _ in range(table_ref.shape[0])]
-        for word, value in enumerate(pick(zero, index, [(table_ref, rows)])):
-            picked_ref[word, :, here] = value
+        for word in range(0, table_ref.shape[0], 2):
+            zero = [jnp.zeros(index.shape, jnp.int32) for _ in range(2)]
+            found = pick(zero, index, [(table_ref, rows)], word)
+            for i, value in enumerate(found):
+                picked_ref[word + i, :, here] = value
     for move in moves:
         move.wait()
 
@@ -124,6 +126,51 @@
     return jnp.concatenate([first, second, tail], axis=0)
 
 
+def fold(values, row):
+    values = list(values) + [None] * (8 - len(values))
+    for half in (4, 2, 1):
+        upper = jnp.bitwise_and(row, half) != 0
+        values = [fold_two(one, two, half, upper) for one, two in zip(values[0::2], values[1::2])]
+    return values[0]
+
+
+def fold_two(one, two, half, upper):
+    if one is None:
+        return None
+    if two is None:
+        return one + across(one, half, upper)
+    return jnp.where(upper, two, one) + across(jnp.where(upper, one, two), half, upper)
+
+
+def across(x, half, upper):
+    if half == 4:
+        return pltpu.roll(x, 4, 0)
+    return jnp.where(upper, pltpu.roll(x, half, 0), pltpu.roll(x, 8 - half, 0))
+
+
+def shuffle(x, index):
+    return lax.gather(
+        x,
+        index[:, :, None],
+        lax.GatherDimensionNumbers(
+            offset_dims=(),
+            collapsed_slice_dims=(0,),
+            start_index_map=(0,),
+            operand_batching_dims=(1,),
+            start_indices_batching_dims=(1,),
+        ),
+        slice_sizes=(1, 1),
+        mode=lax.GatherScatterMode.PROMISE_IN_BOUNDS,
+    )
+
+
+def rows_of(wanted, row):
+    out = jnp.zeros(row.shape, jnp.int32)
+    for s, value in enumerate(wanted):
+        out = jnp.where(row == s, value, out)
+    return out
+
+
 def gram_kernel(shares, count, *refs):
     own_ref, index_ref, weight_ref, ids_ref, picked_ref = refs[:5]
     others, starts = refs[5 : 5 + count], refs[5 + count : 5 + 2 * count]
@@ -138,41 +185,43 @@
     words = picked_ref.shape[0]
     scales = [1.0 / SCALE_WHOLE] * words + [1.0 / SCALE_SPLIT] * (vectors - words)
     half_shares = shares // 2
-    gram = [jnp.zeros((half_shares * 2 * padded, AGG_DEV), jnp.float32) for _ in range(2)]
+    gram = [jnp.zeros((half_shares * 2 * padded, AGG_DEV), jnp.float32) for _ in range(4)]
     step = LANES
+    rows8 = lax.broadcasted_iota(jnp.int32, (8, LANES), 0)
+    place = [4 * (v & 1) + (v & 2) + (v >> 2) for v in range(8)]
+    order = rows_of([place.index(s) for s in range(8)], rows8)
+    listed = pairs + [(0, 0)] * (padded - len(pairs))
+    sides = [
+        tuple(rows_of([place[pair[side]] for pair in listed[at : at + 8]], rows8) for side in range(2))
+        for at in range(0, padded, 8)
+    ]
     for first in range(0, rows, step):
-        pieces = []
-        for start in range(first, first + step, LANES):
-            here = slice(start, start + LANES)
-            weight = weight_ref[:, here]
-            picked = pick([picked_ref[word, :, here] for word in range(words)], index_ref[:, here], tables)
-            smooth = [
-                own_ref[v : v + 1, here] - jnp.sum(weight * value, axis=0, keepdims=True) * scales[v]
-                for v, value in enumerate(decode(picked))
-            ]
-            pieces.append([smooth[p] * smooth[q] for p, q in pairs])
-        zero = jnp.zeros((padded - len(pairs), step), jnp.float32)
-        terms = jnp.concatenate(
-            [jnp.concatenate([half[i] for half in pieces], axis=1) for i in range(len(pairs))] + [zero],
-            axis=0,
-        )
+        here = slice(first, first + step)
+        picked = pick([picked_ref[word, :, here] for word in range(words)], index_ref[:, here], tables)
+        values = [value * scale for value, scale in zip(decode(picked), scales)]
+        near = fold([weight_ref[:, here] * value for value in values], rows8)
+        own = jnp.concatenate([own_ref[:, here], jnp.zeros((8 - vectors, step), jnp.float32)], axis=0)
+        smooth = shuffle(own, order) - near
+        terms = jnp.concatenate([shuffle(smooth, p) * shuffle(smooth, q) for p, q in sides], axis=0)
         coarse = terms.astype(jnp.bfloat16).astype(jnp.float32)
         both = jnp.concatenate([coarse, terms - coarse], axis=0)
-        share = share_of(ids_ref[:, first : first + step], shares)
+        share = jnp.broadcast_to(share_of(ids_ref[:, first : first + step], shares), (2 * padded, step))
         ids = ids_ref[:, first : first + step]
-        within = ids - share * AGG_DEV
+        within = ids - share[:1] * AGG_DEV
         columns = lax.broadcasted_iota(jnp.int32, (AGG_DEV, step), 0)
         one_hot = (columns == within).astype(jnp.float32).astype(jnp.bfloat16)
         for half in range(2):
             masked = jnp.concatenate(
                 [jnp.where(share == half * half_shares + s, both, 0.0) for s in range(half_shares)], axis=0
             ).astype(jnp.bfloat16)
-            gram[half] = gram[half] + lax.dot_general(
+            turn = 2 * (first // step % 2) + half
+            gram[turn] = gram[turn] + lax.dot_general(
                 masked,
                 one_hot,
                 (((1,), (1,)), ((), ())),
                 preferred_element_type=jnp.float32,
             )
+    gram = [gram[half] + gram[2 + half] for half in range(2)]
     for half in range(2):
         for s in range(half_shares):
             at = 2 * padded * s
@@ -183,10 +232,11 @@
 
 def factor_kernel(vectors, parts_ref, factor_ref, spread_ref):
     pairs = pair_list(vectors)
-    total = parts_ref[0]
-    for source in range(1, parts_ref.shape[0]):
-        total = total + parts_ref[source]
-    total = from_wire(total)[:, :AGG_DEV]
+    sums = [parts_ref[source] for source in range(parts_ref.shape[0])]
+    while len(sums) > 1:
+        odd = sums[len(sums) // 2 * 2 :]
+        sums = [one + two for one, two in zip(sums[0::2], sums[1::2])] + odd
+    total = from_wire(sums[0])[:, :AGG_DEV]
     entry = {}
     for i, (p, q) in enumerate(pairs):
         value = total[i : i + 1] * (AGG_DEV / ROWS_DEV)

time: 21.4 us -> 21.3 us (level)
  no operation moved by 1% of the time
where the time goes in v5:
time: 21.3 us; the launch traced here: 21.1 us
  blocking collectives  15.9 us (75%)
  Pallas kernels  3.63 us (17%)
  between operations  0.67 us (3%)
  starting transfers between devices  0.56 us (3%)
  local copies, waits for them, and re-layouts  0.3 us (1%)
    all_to_all x1, blocking collectives, shards(): parts = lax.all_to_all(partial, 'blk', 0, 0, tiled=True)  15.9 us
    pallas_call x1, Pallas kernels, shards(): pl.pallas_call(functools.partial(gram_kernel, shares, len(others)), out_s...  1.68 us
    pallas_call x1, Pallas kernels, shards(): pl.pallas_call(own_kernel, out_shape=[jax.ShapeDtypeStruct(nbr_weight.sha...  1.24 us
    pallas_call x1, Pallas kernels, shards(): pl.pallas_call(functools.partial(factor_kernel, vectors), out_shape=(jax....  0.72 us
    ppermute x1, starting transfers between devices, shards(): others = [lax.ppermute(nullspace, 'grp', [(0, 1), (1, 0)])]  0.56 us
  transfers between devices with their start and end apart: 1, of which 0 were waited for; matrix products, arithmetic and copies ran while one was open for 0% of the time, Pallas kernels for 6%

profile of v5, /device:TPU:0, one launch (start us, length us, event | category | flops | bytes accessed | tf_op | source)
XLA Modules:
  0.0 21.1 jit_solution(12495564656777068484)
XLA Ops:
  0.6 0.0 copy-start
  0.6 0.0 copy-start.1
  0.7 0.6 %collective-permute-start = (f32[6,2048]{1,0:T(8,128)}, f32[6,2048]{1,0:T(8,128)S(1)}, u32[]{:S(2)}, u32[]{:S(2)}) collective-permute-start(f32[6,2048]{1,0:T(8,128)} %refs_0_.1), channel_id=1, source_target_pairs={{0,16},{16,0},{1,17},{17,1},{2,18},{18,2},{3,19},{19,3},{4,20},{20... | collective-permute-start | bytes 147464 | tf_op jit(solution)/shard_map/ppermute | solution.py:273
  1.2 0.3 %copy-done = f32[6,2048]{1,0:T(8,128)S(1)} copy-done((f32[6,2048]{1,0:T(8,128)S(1)}, f32[6,2048]{1,0:T(8,128)}, u32[]{:S(2)}) %copy-start) | copy-done | bytes 49176
  1.5 0.0 copy-done.1
  1.5 1.2 %own.1 = (f32[8,2048]{1,0:T(8,128)S(1)}, s32[1,2048]{1,0:T(1,128)S(1)}, s32[4,8,2048]{2,1,0:T(8,128)S(1)}) custom-call(f32[6,2048]{1,0:T(8,128)S(1)} %copy-done, s32[8,2048]{1,0:T(8,128)S(1)} %copy-done.1, f32[8,2048]{1,0:T(8,128)} %weight_hbm.1, s32[1,2048]{1,0:T(1,128)} %bitcast.3), custom_call_target="tpu_custom_call" | custom-call | flops 4194304 | bytes 262144 | tf_op jit(solution)/shard_map/own/pallas_call | solution.py:286
  2.7 0.0 collective-permute-done.refs_5_
  2.8 1.7 %gram.1 = f32[16,16,128]{2,1,0:T(8,128)S(1)} custom-call(f32[6,2048]{1,0:T(8,128)S(1)} %copy-done, s32[8,2048]{1,0:T(8,128)S(1)} %copy-done.1, f32[8,2048]{1,0:T(8,128)S(1)} %get-tuple-element.7.refs_2_, s32[1,2048]{1,0:T(1,128)S(1)} %get-tuple-element.8.refs_3_, s32[4,8,2048]{2,1,0:T(8,128)S(1)} %get-tuple-element.9.refs_4_, ...), custom_call_target="tpu_custom_call" | custom-call | tf_op jit(solution)/shard_map/gram/pallas_call | solution.py:305
  4.4 15.9 %all_to_all.5.parts_ref = f32[16,16,128]{2,1,0:T(8,128)S(1)} all-to-all(f32[16,16,128]{2,1,0:T(8,128)S(1)} %gram.1), channel_id=1, replica_groups=mesh['grp'=2,'blk'=16] {'blk'}, dimensions={0} | all-to-all | bytes 262144 | tf_op jit(solution)/shard_map/all_to_all | solution.py:314
  20.4 0.7 %factor.1 = (f32[21,96]{1,0:T(8,128)}, f32[1,96]{1,0:T(1,128)}) custom-call(f32[16,16,128]{2,1,0:T(8,128)S(1)} %all_to_all.5.parts_ref), custom_call_target="tpu_custom_call" | custom-call | tf_op jit(solution)/shard_map/factor/pallas_call | solution.py:315
Async XLA Ops:
  0.6 0.8 %copy-start = (f32[6,2048]{1,0:T(8,128)S(1)}, f32[6,2048]{1,0:T(8,128)}, u32[]{:S(2)}) copy-start(f32[6,2048]{1,0:T(8,128)} %refs_0_.1) | copy-start | bytes 147460
  0.6 0.9 %copy-start.1 = (s32[8,2048]{1,0:T(8,128)S(1)}, s32[8,2048]{1,0:T(8,128)}, u32[]{:S(2)}) copy-start(s32[8,2048]{1,0:T(8,128)} %refs_1_.1) | copy-start | bytes 196612
  0.7 2.1 %collective-permute-start = (f32[6,2048]{1,0:T(8,128)}, f32[6,2048]{1,0:T(8,128)S(1)}, u32[]{:S(2)}, u32[]{:S(2)}) collective-permute-start(f32[6,2048]{1,0:T(8,128)} %refs_0_.1), channel_id=1, source_target_pairs={{0,16},{16,0},{1,17},{17,1},{2,18},{18,2},{3,19},{19,3},{4,20},{20... | collective-permute-start | bytes 147464 | tf_op jit(solution)/shard_map/ppermute | solution.py:273

commit v6 on v5

--- a/solution.py
+++ b/solution.py
@@ -77,14 +77,8 @@
     return picked
 
 
-def own_kernel(own_ref, index_ref, weight_hbm, ids_hbm, weight_ref, ids_ref, picked_ref, table_ref, sems):
+def own_kernel(own_ref, index_ref, picked_ref, table_ref):
     rows = own_ref.shape[1]
-    moves = [
-        pltpu.make_async_copy(weight_hbm, weight_ref, sems.at[0]),
-        pltpu.make_async_copy(ids_hbm, ids_ref, sems.at[1]),
-    ]
-    for move in moves:
-        move.start()
     table_ref[...] = encode(own_ref[...])
     for start in range(0, rows, LANES):
         here = slice(start, start + LANES)
@@ -94,8 +88,6 @@
             found = pick(zero, index, [(table_ref, rows)], word)
             for i, value in enumerate(found):
                 picked_ref[word + i, :, here] = value
-    for move in moves:
-        move.wait()
 
 
 def to_wire(gram):
@@ -183,12 +175,12 @@
         table_ref[...] = encode(other_ref[...])
         tables.append((table_ref, start_ref[0]))
     words = picked_ref.shape[0]
-    scales = [1.0 / SCALE_WHOLE] * words + [1.0 / SCALE_SPLIT] * (vectors - words)
     half_shares = shares // 2
     gram = [jnp.zeros((half_shares * 2 * padded, AGG_DEV), jnp.float32) for _ in range(4)]
     step = LANES
     rows8 = lax.broadcasted_iota(jnp.int32, (8, LANES), 0)
     place = [4 * (v & 1) + (v & 2) + (v >> 2) for v in range(8)]
+    unit = jnp.where(rows_of(place, rows8) < words, 1.0 / SCALE_WHOLE, 1.0 / SCALE_SPLIT)
     order = rows_of([place.index(s) for s in range(8)], rows8)
     listed = pairs + [(0, 0)] * (padded - len(pairs))
     sides = [
@@ -198,8 +190,7 @@
     for first in range(0, rows, step):
         here = slice(first, first + step)
         picked = pick([picked_ref[word, :, here] for word in range(words)], index_ref[:, here], tables)
-        values = [value * scale for value, scale in zip(decode(picked), scales)]
-        near = fold([weight_ref[:, here] * value for value in values], rows8)
+        near = fold([weight_ref[:, here] * value for value in decode(picked)], rows8) * unit
         own = jnp.concatenate([own_ref[:, here], jnp.zeros((8 - vectors, step), jnp.float32)], axis=0)
         smooth = shuffle(own, order) - near
         terms = jnp.concatenate([shuffle(smooth, p) * shuffle(smooth, q) for p, q in sides], axis=0)
@@ -268,10 +259,9 @@
     assert len(pairs) == 21 and shares % 2 == 0
     vmem = pl.BlockSpec(memory_space=pltpu.VMEM)
     smem = pl.BlockSpec(memory_space=pltpu.SMEM)
-    hbm = pl.BlockSpec(memory_space=pltpu.HBM)
     if groups == 2:
         others = [lax.ppermute(nullspace, "grp", [(0, 1), (1, 0)])]
-        group = lax.axis_index("grp").astype(jnp.int32)
+        group = jnp.bitwise_xor(lax.axis_index("grp").astype(jnp.int32), 6) * 3
         for n in range(PARITY_STEPS):
             group = group * 3 + 2 * (n + 1)
         group = jnp.bitwise_and(group, 1)
@@ -283,25 +273,16 @@
         ]
         starts = [jnp.zeros((1,), jnp.int32), jnp.full((1,), 2 * rows, jnp.int32)]
     ids = agg_ids.reshape(1, rows)
-    weight, ids, picked = pl.pallas_call(
+    picked = pl.pallas_call(
         own_kernel,
-        out_shape=[
-            jax.ShapeDtypeStruct(nbr_weight.shape, nbr_weight.dtype),
-            jax.ShapeDtypeStruct(ids.shape, ids.dtype),
-            jax.ShapeDtypeStruct((words,) + nbr_index.shape, jnp.int32),
-        ],
-        in_specs=[vmem, vmem, hbm, hbm],
-        out_specs=[vmem] * 3,
-        scratch_shapes=[pltpu.VMEM((words, rows), jnp.int32), pltpu.SemaphoreType.DMA((2,))],
+        out_shape=jax.ShapeDtypeStruct((words,) + nbr_index.shape, jnp.int32),
+        in_specs=[vmem, vmem],
+        out_specs=vmem,
+        scratch_shapes=[pltpu.VMEM((words, rows), jnp.int32)],
         compiler_params=pltpu.CompilerParams(vmem_limit_bytes=4 << 20),
         cost_estimate=pl.CostEstimate(flops=1 << 22, bytes_accessed=1 << 18, transcendentals=0),
         name="own",
-    )(
-        nullspace,
-        nbr_index,
-        pltpu.with_memory_space_constraint(nbr_weight, pltpu.HBM),
-        pltpu.with_memory_space_constraint(ids, pltpu.HBM),
-    )
+    )(nullspace, nbr_index)
     partial = pl.pallas_call(
         functools.partial(gram_kernel, shares, len(others)),
         out_shape=jax.ShapeDtypeStruct((shares, 16, LANES), jnp.float32),
@@ -310,7 +291,7 @@
         scratch_shapes=[pltpu.VMEM((words, rows), jnp.int32) for _ in others],
         compiler_params=pltpu.CompilerParams(vmem_limit_bytes=8 << 20),
         name="gram",
-    )(nullspace, nbr_index, weight, ids, picked, *others, *starts)
+    )(nullspace, nbr_index, nbr_weight, ids, picked, *others, *starts)
     parts = lax.all_to_all(partial, "blk", 0, 0, tiled=True)
     factor, spread = pl.pallas_call(
         functools.partial(factor_kernel, vectors),

time: 21.3 us -> 21.3 us (level)
  no operation moved by 1% of the time
where the time goes in v6:
time: 21.3 us; the launch traced here: 21.1 us
  blocking collectives  15.9 us (75%)
  Pallas kernels  3.6 us (17%)
  between operations  0.68 us (3%)
  starting transfers between devices  0.56 us (3%)
  local copies, waits for them, and re-layouts  0.31 us (1%)
    all_to_all x1, blocking collectives, shards(): parts = lax.all_to_all(partial, 'blk', 0, 0, tiled=True)  15.9 us
    pallas_call x1, Pallas kernels, shards(): pl.pallas_call(functools.partial(gram_kernel, shares, len(others)), out_s...  1.68 us
    pallas_call x1, Pallas kernels, shards(): pl.pallas_call(own_kernel, out_shape=jax.ShapeDtypeStruct((words,) + nbr_...  1.21 us
    pallas_call x1, Pallas kernels, shards(): pl.pallas_call(functools.partial(factor_kernel, vectors), out_shape=(jax....  0.72 us
    ppermute x1, starting transfers between devices, shards(): others = [lax.ppermute(nullspace, 'grp', [(0, 1), (1, 0)])]  0.56 us
  transfers between devices with their start and end apart: 1, of which 0 were waited for; matrix products, arithmetic and copies ran while one was open for 0% of the time, Pallas kernels for 6%

profile of v6, /device:TPU:0, one launch (start us, length us, event | category | flops | bytes accessed | tf_op | source)
XLA Modules:
  0.0 21.1 jit_solution(13012594991001606436)
XLA Ops:
  0.6 0.0 copy-start
  0.6 0.0 copy-start.1
  0.7 0.6 %collective-permute-start = (f32[6,2048]{1,0:T(8,128)}, f32[6,2048]{1,0:T(8,128)S(1)}, u32[]{:S(2)}, u32[]{:S(2)}) collective-permute-start(f32[6,2048]{1,0:T(8,128)} %refs_0_.1), channel_id=1, source_target_pairs={{0,16},{16,0},{1,17},{17,1},{2,18},{18,2},{3,19},{19,3},{4,20},{20... | collective-permute-start | bytes 147464 | tf_op jit(solution)/shard_map/ppermute | solution.py:263
  1.2 0.3 %copy-done = f32[6,2048]{1,0:T(8,128)S(1)} copy-done((f32[6,2048]{1,0:T(8,128)S(1)}, f32[6,2048]{1,0:T(8,128)}, u32[]{:S(2)}) %copy-start) | copy-done | bytes 49176
  1.5 0.0 copy-done.1
  1.5 0.0 copy-start.2
  1.5 0.0 copy-start.3
  1.5 1.2 %own.1.refs_4_ = s32[4,8,2048]{2,1,0:T(8,128)S(1)} custom-call(f32[6,2048]{1,0:T(8,128)S(1)} %copy-done, s32[8,2048]{1,0:T(8,128)S(1)} %copy-done.1), custom_call_target="tpu_custom_call" | custom-call | flops 4194304 | bytes 262144 | tf_op jit(solution)/shard_map/own/pallas_call | solution.py:276
  2.7 0.0 collective-permute-done.refs_5_
  2.7 0.0 copy-done.2
  2.7 0.0 copy-done.3
  2.7 1.7 %gram.1 = f32[16,16,128]{2,1,0:T(8,128)S(1)} custom-call(f32[6,2048]{1,0:T(8,128)S(1)} %copy-done, s32[8,2048]{1,0:T(8,128)S(1)} %copy-done.1, f32[8,2048]{1,0:T(8,128)S(1)} %copy-done.2, s32[1,2048]{1,0:T(1,128)S(1)} %bitcast.3, s32[4,8,2048]{2,1,0:T(8,128)S(1)} %own.1.refs_4_, f32[6,2048]{1,0:T(8,128)S(1)} %collective-permute-done.refs_5_, s32[1]{0:T(128)} %bitcast.1.refs_6_), custom_call_target="tpu_custom_call" | custom-call | tf_op jit(solution)/shard_map/gram/pallas_call | solution.py:286
  4.4 15.9 %all_to_all.5.parts_ref = f32[16,16,128]{2,1,0:T(8,128)S(1)} all-to-all(f32[16,16,128]{2,1,0:T(8,128)S(1)} %gram.1), channel_id=1, replica_groups=mesh['grp'=2,'blk'=16] {'blk'}, dimensions={0} | all-to-all | bytes 262144 | tf_op jit(solution)/shard_map/all_to_all | solution.py:295
  20.4 0.7 %factor.1 = (f32[21,96]{1,0:T(8,128)}, f32[1,96]{1,0:T(1,128)}) custom-call(f32[16,16,128]{2,1,0:T(8,128)S(1)} %all_to_all.5.parts_ref), custom_call_target="tpu_custom_call" | custom-call | tf_op jit(solution)/shard_map/factor/pallas_call | solution.py:296
Async XLA Ops:
  0.6 0.8 %copy-start = (f32[6,2048]{1,0:T(8,128)S(1)}, f32[6,2048]{1,0:T(8,128)}, u32[]{:S(2)}) copy-start(f32[6,2048]{1,0:T(8,128)} %refs_0_.1) | copy-start | bytes 147460
  0.6 0.9 %copy-start.1 = (s32[8,2048]{1,0:T(8,128)S(1)}, s32[8,2048]{1,0:T(8,128)}, u32[]{:S(2)}) copy-start(s32[8,2048]{1,0:T(8,128)} %refs_1_.1) | copy-start | bytes 196612
  0.7 2.1 %collective-permute-start = (f32[6,2048]{1,0:T(8,128)}, f32[6,2048]{1,0:T(8,128)S(1)}, u32[]{:S(2)}, u32[]{:S(2)}) collective-permute-start(f32[6,2048]{1,0:T(8,128)} %refs_0_.1), channel_id=1, source_target_pairs={{0,16},{16,0},{1,17},{17,1},{2,18},{18,2},{3,19},{19,3},{4,20},{20... | collective-permute-start | bytes 147464 | tf_op jit(solution)/shard_map/ppermute | solution.py:263
  1.5 1.2 %copy-start.2 = (f32[8,2048]{1,0:T(8,128)S(1)}, f32[8,2048]{1,0:T(8,128)}, u32[]{:S(2)}) copy-start(f32[8,2048]{1,0:T(8,128)} %refs_2_.1) | copy-start | bytes 196612
  1.5 1.2 %copy-start.3 = (s32[2048]{0:T(1024)S(1)}, s32[2048]{0:T(1024)}, u32[]{:S(2)}) copy-start(s32[2048]{0:T(1024)} %param.5) | copy-start | bytes 24580
